TPU v7x, 256 devices: a whole 4x4x8 slice. The times are simulated.
256 devices in a mesh: band: 16 (over y, x), wall: 16 (over z, core).
Axes of the slice: x: 4, y: 4, z: 8, core: 2. Of those that a mesh axis runs over, the one named last changes fastest.
Arguments:
- state_in: float32 [5, 128, 32, 128], P(None, 'wall', 'band'), may hold values from -8 to 8
- source: float32 [5, 128, 32, 128], P(None, 'wall', 'band'), may hold values from -0.05 to 0.05
- face_flux: float32 [5, 5, 128, 32, 128], P(None, None, 'wall', 'band'), may hold values from -1.6 to 16, as said below
- time_term: float32 [5, 128, 32, 128], P(None, 'wall', 'band'), may hold values from 0.0003 to 0.003
- inplane_coef: float32 [2, 128, 32, 128], P(None, 'wall', 'band'), may hold values from 0.0001 to 0.0006
Outputs:
- state_out: float32 [5, 128, 32, 128], P(None, 'wall', 'band')
Inputs may be any that keep to these rules, and one draw needn't show every extreme that they name: `face_flux`: every 5x5 block is s (G + E) with s > 0 a scale of its cell, G diagonal with entries in 1 to 2, and E zero on the diagonal with entries of magnitude at most 0.2.
All inputs are finite; a program needn't handle non-finite values.
Results may differ from a plain program's by a relative error of at most 0.0003.
Values sent between devices are 32-bit elements; how exact they have to be, the bound alone decides.
A program may use at most 64 MiB of HBM per device.

v0:
```python
import jax
import jax.numpy as jnp
from jax import lax
from jax.sharding import PartitionSpec as P

SWEEPS = 2


def passed_along(block, axis, distance):
    devices = range(lax.axis_size(axis))
    route = [(i - distance, i) for i in devices if i - distance in devices]
    return lax.ppermute(block, axis, route)


def with_halo(cells, sides, width):
    for axis, dim in sides:
        count = lax.axis_size(axis)
        ends = count - 1
        head = lax.slice_in_dim(cells, 0, width, axis=dim)
        tail = lax.slice_in_dim(cells, cells.shape[dim] - width, cells.shape[dim], axis=dim)
        cells = jnp.concatenate(
            [
                lax.ppermute(tail, axis, [(i, (i + 1) % count) for i in range(ends)]),
                cells,
                lax.ppermute(head, axis, [((i + 1) % count, i) for i in range(ends)]),
            ],
            axis=dim,
        )
    return cells


def product(left, right):
    return jnp.sum(left[:, :, None] * right[None, :, :], axis=1)


def apply_blocks(blocks, field):
    return jnp.sum(blocks * field[None, :], axis=1)


def invert(matrix):
    extent = matrix.shape[0]
    identity = jnp.eye(extent, dtype=jnp.float32).reshape(
        (extent, extent) + (1,) * (matrix.ndim - 2)
    )
    working = matrix
    result = jnp.broadcast_to(identity, matrix.shape)
    for pivot in range(extent):
        scale = 1.0 / working[pivot, pivot]
        row_work = working[pivot] * scale
        row_result = result[pivot] * scale
        column = working[:, pivot]
        working = working - column[:, None] * row_work[None]
        result = result - column[:, None] * row_result[None]
        working = working.at[pivot].set(row_work)
        result = result.at[pivot].set(row_result)
    return result


def from_below(array, stride):
    pad_shape = array.shape[:2] + (stride,) + array.shape[3:]
    return jnp.concatenate([jnp.zeros(pad_shape, array.dtype), array[:, :, :-stride]], axis=2)


def from_above(array, stride):
    pad_shape = array.shape[:2] + (stride,) + array.shape[3:]
    return jnp.concatenate([array[:, :, stride:], jnp.zeros(pad_shape, array.dtype)], axis=2)


def cyclic_factor(lower, middle, upper):
    length = middle.shape[2]
    stride = 1
    levels = []
    while stride < length:
        inverse = invert(middle)
        alpha = -product(lower, from_below(inverse, stride))
        gamma = -product(upper, from_above(inverse, stride))
        middle = (
            middle
            + product(alpha, from_below(upper, stride))
            + product(gamma, from_above(lower, stride))
        )
        lower = product(alpha, from_below(lower, stride))
        upper = product(gamma, from_above(upper, stride))
        levels.append((alpha, gamma, stride))
        stride = stride * 2
    return (levels, invert(middle))


def cyclic_apply(levels, final_inverse, target):
    for alpha, gamma, stride in levels:
        target = (
            target
            + product(alpha, from_below(target, stride))
            + product(gamma, from_above(target, stride))
        )
    return product(final_inverse, target)


def segment_setup(lower, middle, upper):
    cells = middle.shape[2]
    layer = jnp.arange(cells)[None, None, :, None]
    inner_lower = jnp.where(layer == 0, 0.0, lower)
    inner_upper = jnp.where(layer == cells - 1, 0.0, upper)
    left_spike = jnp.where(layer == 0, lower, 0.0)
    right_spike = jnp.where(layer == cells - 1, upper, 0.0)
    levels, final_inverse = cyclic_factor(inner_lower, middle, inner_upper)
    spikes = cyclic_apply(levels, final_inverse, jnp.concatenate([left_spike, right_spike], axis=1))
    left_part = spikes[:, :5]
    right_part = spikes[:, 5:]
    packed = jnp.concatenate(
        [left_part[:, :, 0], left_part[:, :, -1], right_part[:, :, 0], right_part[:, :, -1]], axis=1
    )
    every = lax.all_gather(packed[None], "wall", axis=0, tiled=True)
    zero_rows = jnp.zeros_like(every[:, :, 0:5])
    coupling_low = jnp.concatenate(
        [
            jnp.concatenate([zero_rows, every[:, :, 0:5]], axis=2),
            jnp.concatenate([zero_rows, every[:, :, 5:10]], axis=2),
        ],
        axis=1,
    )
    coupling_high = jnp.concatenate(
        [
            jnp.concatenate([every[:, :, 10:15], zero_rows], axis=2),
            jnp.concatenate([every[:, :, 15:20], zero_rows], axis=2),
        ],
        axis=1,
    )
    identity = jnp.eye(10, dtype=jnp.float32)[:, :, None]

    def factor_step(factor_prev, slab):
        low_block, high_block = slab
        inverse = invert(identity - product(low_block, factor_prev))
        factor = product(inverse, high_block)
        return (factor, (factor, inverse))

    _, (factors, inverses) = lax.scan(
        factor_step, jnp.zeros_like(coupling_low[0]), (coupling_low, coupling_high)
    )
    interface_factors = (coupling_low, factors, inverses)
    return (levels, final_inverse, left_part, right_part, interface_factors)


def segment_solve(setup, residual, wall_pos):
    levels, final_inverse, left_part, right_part, interface_factors = setup
    value = cyclic_apply(levels, final_inverse, residual[:, None])[:, 0]
    first_value = value[:, 0]
    last_value = value[:, -1]
    coupling_low, factors, inverses = interface_factors
    packed = jnp.concatenate([first_value[:, None], last_value[:, None]], axis=1)
    every = lax.all_gather(packed[None], "wall", axis=0, tiled=True)
    known = jnp.concatenate([every[:, :, 0], every[:, :, 1]], axis=1)[:, :, None]

    def forward(value_prev, slab):
        low_block, inverse, rhs_block = slab
        solved_value = product(inverse, rhs_block - product(low_block, value_prev))
        return (solved_value, solved_value)

    _, values = lax.scan(forward, jnp.zeros_like(known[0]), (coupling_low, inverses, known))

    def backward(carry, slab):
        factor, solved_value = slab
        result = solved_value - product(factor, carry)
        return (result, result)

    _, interfaces = lax.scan(backward, jnp.zeros_like(values[0]), (factors, values), reverse=True)
    edge_zero = jnp.zeros_like(interfaces[:1])
    padded = jnp.concatenate([edge_zero, interfaces, edge_zero], axis=0)
    window = lax.dynamic_slice_in_dim(padded, wall_pos, 3, 0)
    prev_end = window[0, 5:, 0]
    next_start = window[2, :5, 0]
    return (
        value
        - apply_blocks(left_part, prev_end[:, None])
        - apply_blocks(right_part, next_start[:, None])
    )


def body(state_in, source, face_flux, time_term, inplane_coef):
    cells = face_flux.shape[2]
    lines_i = face_flux.shape[3]
    lines_j = face_flux.shape[4]
    lanes = lines_i * lines_j
    wall_pos = lax.axis_index("wall")
    next_face = passed_along(face_flux[:, :, :1], "wall", -1)
    upper_face = jnp.concatenate([face_flux[:, :, 1:], next_face], axis=2)
    layer = jnp.arange(cells)
    keep = jnp.where((layer == 0) & (wall_pos == 0), 0.0, 1.0).astype(jnp.float32)
    lower = -face_flux * keep[None, None, :, None, None]
    upper = -upper_face
    center = time_term + 2.5 * (inplane_coef[0] + inplane_coef[1])
    identity = jnp.eye(5, dtype=jnp.float32)[:, :, None, None, None]
    middle = face_flux + upper_face + identity * center[:, None]
    flat_shape = (5, 5, cells, lanes)
    setup = segment_setup(
        lower.reshape(flat_shape), middle.reshape(flat_shape), upper.reshape(flat_shape)
    )
    state = state_in
    for sweep in range(SWEEPS):
        padded = with_halo(state, (("wall", 1),), 1)
        wide_i = with_halo(state, (("band", 2),), 2)
        wide_j = jnp.pad(state, ((0, 0), (0, 0), (0, 0), (2, 2)))
        along_i = 1.0 / 12.0 * (wide_i[:, :, 4:] + wide_i[:, :, :-4]) - 4.0 / 3.0 * (
            wide_i[:, :, 3:-1] + wide_i[:, :, 1:-3]
        )
        along_j = 1.0 / 12.0 * (wide_j[:, :, :, 4:] + wide_j[:, :, :, :-4]) - 4.0 / 3.0 * (
            wide_j[:, :, :, 3:-1] + wide_j[:, :, :, 1:-3]
        )
        wall_part = (
            apply_blocks(lower, padded[:, :-2])
            + apply_blocks(middle, state)
            + apply_blocks(upper, padded[:, 2:])
        )
        residual = source - (wall_part + (inplane_coef[0] * along_i + inplane_coef[1] * along_j))
        flat = segment_solve(setup, residual.reshape((5, cells, lanes)), wall_pos)
        delta = flat.reshape((5, cells, lines_i, lines_j))
        state = state + delta
    return state


def solution(mesh):
    return jax.shard_map(
        body,
        mesh=mesh,
        in_specs=(
            P(None, "wall", "band", None),
            P(None, "wall", "band", None),
            P(None, None, "wall", "band", None),
            P(None, "wall", "band", None),
            P(None, "wall", "band", None),
        ),
        out_specs=P(None, "wall", "band", None),
        check_vma=False,
    )
```

profile of v0, /device:TPU:25, one launch (start us, length us, event | category | flops | bytes accessed | tf_op | source)
XLA Modules:
  0.0 324.9 jit_solution(5540001201584545401)
XLA Ops:
  6.5 4.6 %collective-permute-start.3 = (f32[5,8,2,128]{3,2,1,0:T(2,128)}, f32[5,8,2,128]{3,2,1,0:T(2,128)S(1)}, u32[]{:S(2)}, u32[]{:S(2)}) collective-permute-start(f32[5,8,2,128]{3,2,1,0:T(2,128)} %param.125), channel_id=1, source_target_pairs={{16,0},{32,16},{48,32},{64,48},{80,64},{96,80},{112,96},{128,112},... | collective-permute-start | bytes 122888 | tf_op jit(solution)/shard_map/ppermute | solution.py:25
  11.1 1.9 collective-permute-start.4
  13.8 4.4 %collective-permute-start.1 = (f32[5,1,2,128]{3,2,1,0:T(2,128)S(1)}, f32[5,1,2,128]{3,2,1,0:T(2,128)S(1)}, u32[]{:S(2)}, u32[]{:S(2)}) collective-permute-start(f32[5,1,2,128]{3,2,1,0:T(2,128)S(1)} %get-tuple-element.1500), channel_id=1, source_target_pairs={{0,1},{1,2},{2,3},{3,4},{4,5},{5,6},{6,7},{7,8},{8,9},{9,10},{10,1... | collective-permute-start | bytes 15368 | tf_op jit(solution)/shard_map/ppermute | solution.py:23
  18.2 1.9 collective-permute-start.2
  20.8 1.9 collective-permute-start
  26.4 1.5 multiply_reduce_fusion.47
  39.0 20.5 %all-gather.1 = f32[80,2,256]{2,1,0:T(2,128)S(1)} all-gather(f32[5,2,256]{2,1,0:T(2,128)S(1)} %pad_maximum_fusion.11), channel_id=3, replica_groups=mesh['band'=16,'wall'=16] {'wall'}, dimensions={0}, use_global_device_ids=true | all-gather | bytes 174080 | tf_op jit(solution)/shard_map/all_gather | solution.py:151
  60.3 22.5 %all-gather.5.cloned.1.call-done = f32[80,20,256]{2,1,0:T(8,128)} async-done(((f32[5,20,256]{2,1,0:T(8,128)}), f32[80,20,256]{2,1,0:T(8,128)}) %all-gather.5.cloned.1.call-update) | async-done | bytes 1638416 | tf_op jit(solution)/shard_map/all_gather | solution.py:113
  82.8 2.7 fusion.159
  85.5 1.8 select_maximum_fusion
  87.7 55.5 %while.133 = (s32[]{:T(128)}, f32[10,10,256]{2,1,0:T(8,128)S(1)}, f32[16,10,10,256]{3,2,1,0:T(8,128)}, f32[16,10,10,256]{3,2,1,0:T(8,128)}, f32[16,10,10,256]{3,...) while((s32[]{:T(128)}, f32[10,10,256]{2,1,0:T(8,128)S(1)}, ...), condition=%wide.region_36.37_spmd.clone, body=%wide.region_33.36_spmd.clone.sunk | while | flops 2097072 | bytes 7286901 | solution.py:137
  144.0 40.6 %while.131 = (s32[]{:T(128)}, f32[10,1,256]{2,0,1:T(8,128)S(1)}, f32[16,10,1,256]{3,2,1,0:T(1,128)}, f32[16,10,10,256]{3,2,1,0:T(8,128)}, f32[16,10,1,256]{3,0,1...) while((s32[]{:T(128)}, f32[10,1,256]{2,0,1:T(8,128)S(1)}, f32[16,10,1,256]{3,2,1,0:T(1,128)}, ...), condition=%wide.region_40.41_spmd, body=%wide.region_37.40_spmd.sunk | while | flops 99842 | bytes 318041 | solution.py:159
  185.3 37.2 %while.134 = (s32[]{:T(128)}, f32[10,1,256]{2,1,0:T(1,128)S(1)}, f32[16,10,1,256]{3,1,2,0:T(8,128)}, f32[16,10,1,256]{3,2,1,0:T(1,128)}, f32[16,10,10,256]{3,2,1,0:T(8,128)}, /*index=5*/s32[]{:T(128)}, s32[]{:T(128)}, s32[]{:T(128)}) while((s32[]{:T(128)}, f32[10,1,256]{2,1,0:T(1,128)S(1)}, f32[16,10,1,256]{3,1,2,0:T(8,128)}, ...), condition=%wide.region_43.44_spmd.clone, body=%wide.region_41.43_spmd.clone.sunk | while | flops 56324 | bytes 241783 | solution.py:166
  224.2 2.7 collective-permute-start.5
  226.9 1.9 collective-permute-start.6
  229.8 4.6 %collective-permute-start.7 = (f32[5,8,2,128]{3,2,1,0:T(2,128)S(1)}, f32[5,8,2,128]{3,2,1,0:T(2,128)S(1)}, u32[]{:S(2)}, u32[]{:S(2)}) collective-permute-start(f32[5,8,2,128]{3,2,1,0:T(2,128)S(1)} %copy_add_fusion.1), channel_id=1, source_target_pairs={{16,0},{32,16},{48,32},{64,48},{80,64},{96,80},{112,96},{128,112},... | collective-permute-start | bytes 122888 | tf_op jit(solution)/shard_map/ppermute | solution.py:25
  234.4 1.9 collective-permute-start.8
  237.4 1.1 multiply_reduce_fusion.36
  238.5 3.0 collective-permute-done.8
  241.4 1.7 add_subtract_fusion
  243.9 1.4 broadcast_in_dim_reshape.12
  249.6 18.3 %all-gather.2 = f32[80,2,256]{2,1,0:T(2,128)S(1)} all-gather(f32[5,2,256]{2,1,0:T(2,128)S(1)} %pad_maximum_fusion.12), channel_id=4, replica_groups=mesh['band'=16,'wall'=16] {'wall'}, dimensions={0}, use_global_device_ids=true | all-gather | bytes 174080 | tf_op jit(solution)/shard_map/all_gather | solution.py:151
  268.8 31.5 %while.132 = (s32[]{:T(128)}, f32[10,1,256]{2,0,1:T(8,128)S(1)}, f32[16,10,1,256]{3,2,1,0:T(1,128)S(1)}, f32[16,10,10,256]{3,2,1,0:T(8,128)}, f32[16,10,1,256]{3...) while((s32[]{:T(128)}, f32[10,1,256]{2,0,1:T(8,128)S(1)}, f32[16,10,1,256]{3,2,1,0:T(1,128)S(1)}, ...), condition=%wide.region_59.60_spmd, body=%wide.region_56.59_spmd.sunk | while | flops 99842 | bytes 323677 | solution.py:159
  300.3 16.9 %while.135 = (s32[]{:T(128)}, f32[10,1,256]{2,1,0:T(1,128)S(1)}, f32[16,10,1,256]{3,1,2,0:T(8,128)S(1)}, f32[16,10,1,256]{3,2,1,0:T(1,128)S(1)}, f32[16,10,10,25...) while((s32[]{:T(128)}, f32[10,1,256]{2,1,0:T(1,128)S(1)}, ...), condition=%wide.region_62.63_spmd.clone, body=%wide.region_60.62_spmd.clone.sunk | while | flops 56324 | bytes 247927 | solution.py:166
  (1754 shorter events, 199.4 us)
Async XLA Ops:
  6.5 76.2 %all-gather.5.cloned.1.call-start = ((), (), s32[]{:S(2)}) async-start(), calls=%async_computation | async-start | bytes 2088960 | tf_op jit(solution)/shard_map/all_gather | solution.py:113
  6.5 23.4 %collective-permute-start.3 = (f32[5,8,2,128]{3,2,1,0:T(2,128)}, f32[5,8,2,128]{3,2,1,0:T(2,128)S(1)}, u32[]{:S(2)}, u32[]{:S(2)}) collective-permute-start(f32[5,8,2,128]{3,2,1,0:T(2,128)} %param.125), channel_id=1, source_target_pairs={{16,0},{32,16},{48,32},{64,48},{80,64},{96,80},{112,96},{128,112},... | collective-permute-start | bytes 122888 | tf_op jit(solution)/shard_map/ppermute | solution.py:25
  11.1 18.8 %collective-permute-start.4 = (f32[5,8,2,128]{3,2,1,0:T(2,128)}, f32[5,8,2,128]{3,2,1,0:T(2,128)S(1)}, u32[]{:S(2)}, u32[]{:S(2)}) collective-permute-start(f32[5,8,2,128]{3,2,1,0:T(2,128)} %param.125), channel_id=1, source_target_pairs={{0,16},{16,32},{32,48},{48,64},{64,80},{80,96},{96,112},{112,128},... | collective-permute-start | bytes 122888 | tf_op jit(solution)/shard_map/ppermute | solution.py:23
  13.8 11.7 %collective-permute-start.1 = (f32[5,1,2,128]{3,2,1,0:T(2,128)S(1)}, f32[5,1,2,128]{3,2,1,0:T(2,128)S(1)}, u32[]{:S(2)}, u32[]{:S(2)}) collective-permute-start(f32[5,1,2,128]{3,2,1,0:T(2,128)S(1)} %get-tuple-element.1500), channel_id=1, source_target_pairs={{0,1},{1,2},{2,3},{3,4},{4,5},{5,6},{6,7},{7,8},{8,9},{9,10},{10,1... | collective-permute-start | bytes 15368 | tf_op jit(solution)/shard_map/ppermute | solution.py:23
  18.2 7.3 %collective-permute-start.2 = (f32[5,1,2,128]{3,2,1,0:T(2,128)S(1)}, f32[5,1,2,128]{3,2,1,0:T(2,128)S(1)}, u32[]{:S(2)}, u32[]{:S(2)}) collective-permute-start(f32[5,1,2,128]{3,2,1,0:T(2,128)S(1)} %get-tuple-element.1499), channel_id=1, source_target_pairs={{1,0},{2,1},{3,2},{4,3},{5,4},{6,5},{7,6},{8,7},{9,8},{10,9},{11,1... | collective-permute-start | bytes 15368 | tf_op jit(solution)/shard_map/ppermute | solution.py:25
  20.8 5.6 %collective-permute-start = (f32[5,5,1,2,128]{4,3,2,1,0:T(2,128)S(1)}, f32[5,5,1,2,128]{4,3,2,1,0:T(2,128)S(1)}, u32[]{:S(2)}, u32[]{:S(2)}) collective-permute-start(f32[5,5,1,2,128]{4,3,2,1,0:T(2,128)S(1)} %slice.2125), channel_id=1, source_target_pairs={{1,0},{2,1},{3,2},{4,3},{5,4},{6,5},{7,6},{8,7},{9,8},{10,9},{11,1... | collective-permute-start | bytes 76808 | tf_op jit(solution)/shard_map/ppermute | solution.py:12
  23.5 6.4 %copy-start.17 = (f32[8,2,128]{2,1,0:T(2,128)}, f32[8,2,128]{2,1,0:T(2,128)S(1)}, u32[]{:S(2)}) copy-start(f32[8,2,128]{2,1,0:T(2,128)S(1)} %get-tuple-element.1533) | copy-start | bytes 24580
  23.5 6.4 %copy-start.18 = (f32[8,2,128]{2,1,0:T(2,128)}, f32[8,2,128]{2,1,0:T(2,128)S(1)}, u32[]{:S(2)}) copy-start(f32[8,2,128]{2,1,0:T(2,128)S(1)} %get-tuple-element.1534) | copy-start | bytes 24580
  25.3 3.4 %copy-start = (f32[5,5,7,2,128]{4,3,2,1,0:T(2,128)}, f32[5,5,7,2,128]{4,3,2,1,0:T(2,128)S(1)}, u32[]{:S(2)}) copy-start(f32[5,5,7,2,128]{4,3,2,1,0:T(2,128)S(1)} %slice.2124) | copy-start | bytes 537604
  26.4 2.7 copy-start.13
  27.9 0.9 copy-start.2
  27.9 1.0 copy-start.3
  29.4 1.2 copy-start.4
  29.5 0.8 copy-start.12
  29.5 0.8 copy-start.16
  29.6 1.1 copy-start.5
  144.0 92.5 %copy-start.1 = (f32[5,5,7,2,128]{4,3,2,1,0:T(2,128)S(1)}, f32[5,5,7,2,128]{4,3,2,1,0:T(2,128)}, u32[]{:S(2)}) copy-start(f32[5,5,7,2,128]{4,3,2,1,0:T(2,128)} %copy-done) | copy-start | bytes 537604
  224.2 12.2 %collective-permute-start.5 = (f32[5,1,2,128]{3,2,1,0:T(2,128)S(1)}, f32[5,1,2,128]{3,2,1,0:T(2,128)S(1)}, u32[]{:S(2)}, u32[]{:S(2)}) collective-permute-start(f32[5,1,2,128]{3,2,1,0:T(2,128)S(1)} %get-tuple-element.1487), channel_id=1, source_target_pairs={{0,1},{1,2},{2,3},{3,4},{4,5},{5,6},{6,7},{7,8},{8,9},{9,10},{10,1... | collective-permute-start | bytes 15368 | tf_op jit(solution)/shard_map/ppermute | solution.py:23
  226.9 9.5 %collective-permute-start.6 = (f32[5,1,2,128]{3,2,1,0:T(2,128)S(1)}, f32[5,1,2,128]{3,2,1,0:T(2,128)S(1)}, u32[]{:S(2)}, u32[]{:S(2)}) collective-permute-start(f32[5,1,2,128]{3,2,1,0:T(2,128)S(1)} %get-tuple-element.1488), channel_id=1, source_target_pairs={{1,0},{2,1},{3,2},{4,3},{5,4},{6,5},{7,6},{8,7},{9,8},{10,9},{11,1... | collective-permute-start | bytes 15368 | tf_op jit(solution)/shard_map/ppermute | solution.py:25
  229.8 8.6 %collective-permute-start.7 = (f32[5,8,2,128]{3,2,1,0:T(2,128)S(1)}, f32[5,8,2,128]{3,2,1,0:T(2,128)S(1)}, u32[]{:S(2)}, u32[]{:S(2)}) collective-permute-start(f32[5,8,2,128]{3,2,1,0:T(2,128)S(1)} %copy_add_fusion.1), channel_id=1, source_target_pairs={{16,0},{32,16},{48,32},{64,48},{80,64},{96,80},{112,96},{128,112},... | collective-permute-start | bytes 122888 | tf_op jit(solution)/shard_map/ppermute | solution.py:25
  234.4 7.0 %collective-permute-start.8 = (f32[5,8,2,128]{3,2,1,0:T(2,128)S(1)}, f32[5,8,2,128]{3,2,1,0:T(2,128)S(1)}, u32[]{:S(2)}, u32[]{:S(2)}) collective-permute-start(f32[5,8,2,128]{3,2,1,0:T(2,128)S(1)} %copy_add_fusion.1), channel_id=1, source_target_pairs={{0,16},{16,32},{32,48},{48,64},{64,80},{80,96},{96,112},{112,128},... | collective-permute-start | bytes 122888 | tf_op jit(solution)/shard_map/ppermute | solution.py:23
  237.3 11.0 %copy-start.8 = (f32[5,5,8,256]{3,2,1,0:T(8,128)S(1)}, f32[5,5,8,256]{3,2,1,0:T(8,128)}, u32[]{:S(2)}) copy-start(f32[5,5,8,256]{3,2,1,0:T(8,128)} %copy-done.7) | copy-start | bytes 614404
  245.3 4.1 %copy-start.11 = (f32[5,5,8,256]{3,2,1,0:T(8,128)S(1)}, f32[5,5,8,256]{3,2,1,0:T(8,128)}, u32[]{:S(2)}) copy-start(f32[5,5,8,256]{3,2,1,0:T(8,128)} %copy-done.10) | copy-start | bytes 614404
  245.3 4.2 %copy-start.15 = (f32[5,8,256]{2,1,0:T(8,128)S(1)}, f32[5,8,256]{2,1,0:T(8,128)}, u32[]{:S(2)}) copy-start(f32[5,8,256]{2,1,0:T(8,128)} %broadcast_in_dim_reshape.12) | copy-start | bytes 122884
  (5 other events, 3.5 us)
Sparse Core Ops, SparseCore 0:
  38.4 44.3 all-gather.4
where the time goes:
time: 330 us; the launch traced here: 325 us
  other arithmetic  128 us (39%)
  local copies, waits for them, and re-layouts  81.7 us (25%)
  blocking collectives  38.7 us (12%)
  starting transfers between devices  25.8 us (8%)
  waiting for transfers between devices  25.5 us (8%)
  between operations  15.3 us (5%)
  loops' own time  9.92 us (3%)
    reduce_sum x161, other arithmetic, product(): return jnp.sum(left[:, :, None] * right[None, :, :], axis=1)  73.9 us
    all_gather x2, blocking collectives, segment_solve(): every = lax.all_gather(packed[None], 'wall', axis=0, tiled=True)  38.7 us
    dynamic_slice x32, local copies, waits for them, and re-layouts, segment_solve(): lax.scan(forward, jnp.zeros_like(known[0]), (coupling_low, inverses, known))  29 us
    all_gather x1, waiting for transfers between devices, segment_setup(): every = lax.all_gather(packed[None], 'wall', axis=0, tiled=True)  22.5 us
    mul x43, local copies, waits for them, and re-layouts, product(): return jnp.sum(left[:, :, None] * right[None, :, :], axis=1)  15.2 us
    ppermute x4, starting transfers between devices, with_halo(): lax.ppermute(head, axis, [((i + 1) % count, i) for i in range(ends)])  13 us
    dynamic_update_slice x16, local copies, waits for them, and re-layouts, segment_setup(): lax.scan(factor_step, jnp.zeros_like(coupling_low[0]), (coupling_low, cou...  12.3 us
    sub x32, other arithmetic, backward(): result = solved_value - product(factor, carry)  11.9 us
  transfers between devices with their start and end apart: 10, of which 2 were waited for; matrix products, arithmetic and copies ran while one was open for 4% of the time, Pallas kernels for 0%

commit v1 on v0

v1 whole, which is shorter than its diff:
```python
import jax
import jax.numpy as jnp
from jax import lax
from jax.experimental import pallas as pl
from jax.experimental.pallas import tpu as pltpu
from jax.sharding import PartitionSpec as P

SWEEPS = 2
N = 5
CELLS = 8
INNER = CELLS - 1
SEGS = 16
MATRIX_GROUPS = 13
VECTOR_GROUPS = 2
MATRIX_ROWS = 16
VECTOR_ROWS = 8
MESH = pl.DeviceIdType.MESH


def matmul(left, right):
    total = left[:, 0:1] * right[0:1]
    for k in range(1, N):
        total = total + left[:, k : k + 1] * right[k : k + 1]
    return total


def matvec(matrix, vector):
    total = matrix[:, 0] * vector[0:1]
    for k in range(1, N):
        total = total + matrix[:, k] * vector[k : k + 1]
    return total


def with_entry(row, at, value):
    parts = []
    if at > 0:
        parts.append(row[:at])
    parts.append(value)
    if at < N - 1:
        parts.append(row[at + 1 :])
    return jnp.concatenate(parts, axis=0)


def invert(matrix):
    rows = [matrix[i] for i in range(N)]
    zero = jnp.zeros_like(rows[0][0:1])
    for p in range(N):
        scale = 1.0 / rows[p][p : p + 1]
        pivot_row = with_entry(rows[p] * scale, p, scale)
        updated = []
        for i in range(N):
            if i == p:
                updated.append(pivot_row)
            else:
                column = rows[i][p : p + 1]
                updated.append(with_entry(rows[i], p, zero) - column * pivot_row)
        rows = updated
    return jnp.stack(rows, axis=0)


def add_diagonal(matrix, diagonal):
    rows = [
        with_entry(matrix[i], i, matrix[i][i : i + 1] + diagonal[i : i + 1]) for i in range(N)
    ]
    return jnp.stack(rows, axis=0)


def one_minus(matrix):
    rows = [with_entry(-matrix[i], i, 1.0 - matrix[i][i : i + 1]) for i in range(N)]
    return jnp.stack(rows, axis=0)


def swap_rows(values):
    return jnp.concatenate([values[..., 1:2, :], values[..., 0:1, :]], axis=-2)


def lane_roll(values, shift):
    return pltpu.roll(values, shift % 128, values.ndim - 1)


def lane_of(values):
    return lax.broadcasted_iota(jnp.int32, values.shape, values.ndim - 1)


def row_of(values):
    return lax.broadcasted_iota(jnp.int32, values.shape, values.ndim - 2)


def segment_before(values, distance):
    if distance == 8:
        return swap_rows(values)
    rolled = lane_roll(values, 16 * distance)
    return jnp.where(lane_of(values) < 16 * distance, swap_rows(rolled), rolled)


def segment_after(values, distance):
    if distance == 8:
        return swap_rows(values)
    rolled = lane_roll(values, -16 * distance)
    return jnp.where(lane_of(values) >= 128 - 16 * distance, swap_rows(rolled), rolled)


def first_segment(values):
    return (row_of(values) == 0) & (lane_of(values) < 16)


def last_segment(values):
    return (row_of(values) == 1) & (lane_of(values) >= 112)


def transpose_groups(tile):
    sublane = row_of(tile)
    group = lane_of(tile) // 16
    for bit in (1, 2, 4):
        in_row = (sublane // bit) % 2 == 1
        in_lane = (group // bit) % 2 == 1
        from_next = lane_roll(pltpu.roll(tile, 8 - bit, 0), 16 * bit)
        if bit == 4:
            other = from_next
        else:
            from_prev = lane_roll(pltpu.roll(tile, bit, 0), -16 * bit)
            other = jnp.where(in_lane, from_next, from_prev)
        tile = jnp.where(in_row == in_lane, tile, other)
    return tile


def pack(fields, messages, groups, rows):
    for g in range(groups):
        for r in range(2):
            tile = fields[pl.ds(16 * g + r, 8, stride=2), :]
            messages[pl.ds(8 * r * rows + g, 8, stride=rows), :] = transpose_groups(tile)


def unpack(messages, fields, groups, rows):
    for g in range(groups):
        for r in range(2):
            tile = messages[pl.ds(8 * r * rows + g, 8, stride=rows), :]
            fields[pl.ds(16 * g + r, 8, stride=2), :] = transpose_groups(tile)


def put_vector(fields, first, vector):
    for i in range(N):
        at = 2 * (first + i)
        fields[at : at + 2, :] = vector[i]


def get_vector(fields, first):
    return jnp.stack([fields[2 * (first + i) : 2 * (first + i) + 2, :] for i in range(N)], axis=0)


def put_matrix(fields, first, matrix):
    for i in range(N):
        put_vector(fields, first + N * i, matrix[i])


def get_matrix(fields, first):
    return jnp.stack([get_vector(fields, first + N * i) for i in range(N)], axis=0)


def kernel(
    state_in,
    source_in,
    face_in,
    time_in,
    coef_in,
    out,
    state,
    source,
    face,
    time,
    coef,
    held_inverse,
    held_lower,
    held_upper,
    spike_low,
    spike_high,
    partial,
    chain_inverse,
    round_inverse,
    round_lower,
    round_upper,
    matrix_fields,
    vector_fields,
    matrix_out,
    matrix_in,
    vector_out,
    vector_in,
    halo_in,
    load_sem,
    matrix_send,
    matrix_recv,
    vector_send,
    vector_recv,
    halo_send,
    halo_recv,
):
    wall = lax.axis_index("wall")
    band = lax.axis_index("band")
    bands = lax.axis_size("band")
    band_prev = lax.rem(band + bands - 1, bands)
    band_next = lax.rem(band + 1, bands)

    barrier = pltpu.get_barrier_semaphore()
    for neighbour in (band_prev, band_next):
        pl.semaphore_signal(barrier, inc=1, device_id={"band": neighbour}, device_id_type=MESH)
    for offset in range(1, SEGS):
        pl.semaphore_signal(
            barrier,
            inc=1,
            device_id={"wall": lax.rem(wall + offset, SEGS)},
            device_id_type=MESH,
        )

    loads = [
        pltpu.make_async_copy(face_in, face, load_sem.at[0]),
        pltpu.make_async_copy(time_in, time, load_sem.at[1]),
        pltpu.make_async_copy(coef_in, coef, load_sem.at[2]),
        pltpu.make_async_copy(state_in, state, load_sem.at[3]),
        pltpu.make_async_copy(source_in, source, load_sem.at[4]),
    ]
    for load in loads:
        load.start()

    def exchange(send_from, land_in, send_sems, recv_sems, rows):
        copies = []
        for offset in range(1, SEGS):
            there = lax.rem(wall + offset, SEGS)
            copy = pltpu.make_async_remote_copy(
                src_ref=send_from.at[pl.ds(pl.multiple_of(there * rows, rows), rows)],
                dst_ref=land_in.at[pl.ds(pl.multiple_of(wall * rows, rows), rows)],
                send_sem=send_sems.at[offset],
                recv_sem=recv_sems.at[offset],
                device_id={"wall": there},
                device_id_type=MESH,
            )
            copy.start()
            copies.append(copy)
        own = pl.ds(pl.multiple_of(wall * rows, rows), rows)
        land_in[own, :] = send_from[own, :]
        return copies

    def exchange_halo(turn):
        copies = []
        for side, there in ((0, band_next), (1, band_prev)):
            copy = pltpu.make_async_remote_copy(
                src_ref=state,
                dst_ref=halo_in.at[turn, side],
                send_sem=halo_send.at[turn, side],
                recv_sem=halo_recv.at[turn, side],
                device_id={"band": there},
                device_id_type=MESH,
            )
            copy.start()
            copies.append(copy)
        return copies

    for load in loads[:3]:
        load.wait()

    upper = None
    spike = None
    for m in range(INNER):
        own_face = face[:, :, m]
        next_face = face[:, :, m + 1]
        center = time[:, m] + 2.5 * (coef[0:1, m] + coef[1:2, m])
        if m == 0:
            pivot = own_face + next_face
        else:
            pivot = next_face + matmul(own_face, one_minus(upper))
        inverse = invert(add_diagonal(pivot, center))
        lower = matmul(inverse, own_face)
        upper = matmul(inverse, next_face)
        spike = lower if m == 0 else matmul(lower, spike)
        held_inverse[m] = inverse
        held_lower[m] = lower
        held_upper[m] = upper
        spike_low[m] = spike
    spike_high[INNER - 1] = upper
    high = upper
    for m in range(INNER - 2, -1, -1):
        upper = held_upper[m]
        spike = spike_low[m] + matmul(upper, spike)
        high = matmul(upper, high)
        spike_low[m] = spike
        spike_high[m] = high

    first_face = face[:, :, 0]
    last_face = face[:, :, INNER]
    center = time[:, INNER] + 2.5 * (coef[0:1, INNER] + coef[1:2, INNER])
    put_matrix(matrix_fields, 0, matmul(first_face, one_minus(spike)))
    put_matrix(matrix_fields, 25, -matmul(first_face, high))
    put_matrix(matrix_fields, 50, -matmul(last_face, spike_low[INNER - 1]))
    put_matrix(
        matrix_fields,
        75,
        add_diagonal(matmul(last_face, one_minus(spike_high[INNER - 1])), center),
    )

    for load in loads[3:]:
        load.wait()
    pl.semaphore_wait(barrier, SEGS + 1)
    pending = exchange_halo(0)
    pack(matrix_fields, matrix_out, MATRIX_GROUPS, MATRIX_ROWS)
    matrix_copies = exchange(matrix_out, matrix_in, matrix_send, matrix_recv, MATRIX_ROWS)

    has_prev = jnp.where(band > 0, 1.0, 0.0).astype(jnp.float32)
    has_next = jnp.where(band < bands - 1, 1.0, 0.0).astype(jnp.float32)

    def eliminate(turn):
        value = None
        for m in range(CELLS):
            here = state[:, m]
            before = halo_in[turn, 0, :, m] * has_prev
            after = halo_in[turn, 1, :, m] * has_next
            top = row_of(here) == 0
            along_i = (1.0 / 12.0) * (before + after) - (4.0 / 3.0) * swap_rows(
                here + jnp.where(top, after, before)
            )
            lane = lane_of(here)
            far = jnp.where(lane < 126, lane_roll(here, -2), 0.0) + jnp.where(
                lane >= 2, lane_roll(here, 2), 0.0
            )
            near = jnp.where(lane < 127, lane_roll(here, -1), 0.0) + jnp.where(
                lane >= 1, lane_roll(here, 1), 0.0
            )
            along_j = (1.0 / 12.0) * far - (4.0 / 3.0) * near
            target = source[:, m] - (coef[0:1, m] * along_i + coef[1:2, m] * along_j)
            if m == INNER:
                put_vector(vector_fields, N, target + matvec(face[:, :, INNER], value))
            else:
                fresh = matvec(held_inverse[m], target)
                value = fresh if m == 0 else fresh + matvec(held_lower[m], value)
                partial[m] = value
        for m in range(INNER - 2, -1, -1):
            value = partial[m] + matvec(held_upper[m], value)
            partial[m] = value
        put_vector(vector_fields, 0, matvec(face[:, :, 0], value))

    def factor_chain():
        from_above = []
        for first in (0, 25):
            block = segment_after(get_matrix(matrix_fields, first), 1)
            from_above.append(jnp.where(last_segment(block), 0.0, block))
        lower = get_matrix(matrix_fields, 50)
        lower = jnp.where(first_segment(lower), 0.0, lower)
        inverse = invert(get_matrix(matrix_fields, 75) + from_above[0])
        chain_inverse[...] = inverse
        lower = matmul(inverse, lower)
        upper = matmul(inverse, from_above[1])
        for step, distance in enumerate((1, 2, 4, 8)):
            upper_before = segment_before(upper, distance)
            lower_after = segment_after(lower, distance)
            inverse = invert(
                one_minus(matmul(lower, upper_before) + matmul(upper, lower_after))
            )
            low = matmul(inverse, lower)
            high = matmul(inverse, upper)
            round_inverse[step] = inverse
            round_lower[step] = low
            round_upper[step] = high
            if distance < 8:
                lower = -matmul(low, segment_before(lower, distance))
                upper = -matmul(high, segment_after(upper, distance))

    def solve_chain():
        from_above = segment_after(get_vector(vector_fields, 0), 1)
        from_above = jnp.where(last_segment(from_above), 0.0, from_above)
        value = matvec(chain_inverse[...], get_vector(vector_fields, N) + from_above)
        for step, distance in enumerate((1, 2, 4, 8)):
            value = (
                matvec(round_inverse[step], value)
                - matvec(round_lower[step], segment_before(value, distance))
                - matvec(round_upper[step], segment_after(value, distance))
            )
        before = segment_before(value, 1)
        put_vector(vector_fields, 0, jnp.where(first_segment(before), 0.0, before))
        put_vector(vector_fields, N, value)

    for turn in range(SWEEPS):
        for copy in pending:
            copy.wait()
        eliminate(turn)
        trips = []
        trip = 2 * turn
        pack(vector_fields, vector_out.at[trip], VECTOR_GROUPS, VECTOR_ROWS)
        trips.append(
            exchange(
                vector_out.at[trip],
                vector_in.at[trip],
                vector_send.at[trip],
                vector_recv.at[trip],
                VECTOR_ROWS,
            )
        )
        if turn == 0:
            for copy in matrix_copies:
                copy.wait()
            unpack(matrix_in, matrix_fields, MATRIX_GROUPS, MATRIX_ROWS)
            factor_chain()
        for copy in trips[0]:
            copy.wait()
        unpack(vector_in.at[trip], vector_fields, VECTOR_GROUPS, VECTOR_ROWS)
        solve_chain()
        trip = trip + 1
        pack(vector_fields, vector_out.at[trip], VECTOR_GROUPS, VECTOR_ROWS)
        answers = exchange(
            vector_out.at[trip],
            vector_in.at[trip],
            vector_send.at[trip],
            vector_recv.at[trip],
            VECTOR_ROWS,
        )
        for copy in answers:
            copy.wait()
        unpack(vector_in.at[trip], vector_fields, VECTOR_GROUPS, VECTOR_ROWS)
        below = get_vector(vector_fields, 0)
        own = get_vector(vector_fields, N)
        target = out if turn == SWEEPS - 1 else state
        for m in range(INNER):
            target[:, m] = partial[m] + matvec(spike_low[m], below) + matvec(spike_high[m], own)
        target[:, INNER] = own
        if turn < SWEEPS - 1:
            pending = exchange_halo(turn + 1)


def body(state_in, source, face_flux, time_term, inplane_coef):
    f32 = jnp.float32
    cell = (2, 128)
    anywhere = pl.BlockSpec(memory_space=pl.ANY)
    return pl.pallas_call(
        kernel,
        out_shape=jax.ShapeDtypeStruct(state_in.shape, f32),
        in_specs=[anywhere] * 5,
        out_specs=pl.BlockSpec(memory_space=pltpu.VMEM),
        scratch_shapes=[
            pltpu.VMEM((N, CELLS) + cell, f32),
            pltpu.VMEM((N, CELLS) + cell, f32),
            pltpu.VMEM((N, N, CELLS) + cell, f32),
            pltpu.VMEM((N, CELLS) + cell, f32),
            pltpu.VMEM((2, CELLS) + cell, f32),
            pltpu.VMEM((INNER, N, N) + cell, f32),
            pltpu.VMEM((INNER, N, N) + cell, f32),
            pltpu.VMEM((INNER, N, N) + cell, f32),
            pltpu.VMEM((INNER, N, N) + cell, f32),
            pltpu.VMEM((INNER, N, N) + cell, f32),
            pltpu.VMEM((INNER, N) + cell, f32),
            pltpu.VMEM((N, N) + cell, f32),
            pltpu.VMEM((4, N, N) + cell, f32),
            pltpu.VMEM((4, N, N) + cell, f32),
            pltpu.VMEM((4, N, N) + cell, f32),
            pltpu.VMEM((16 * MATRIX_GROUPS, 128), f32),
            pltpu.VMEM((16 * VECTOR_GROUPS, 128), f32),
            pltpu.VMEM((SEGS * MATRIX_ROWS, 128), f32),
            pltpu.VMEM((SEGS * MATRIX_ROWS, 128), f32),
            pltpu.VMEM((2 * SWEEPS, SEGS * VECTOR_ROWS, 128), f32),
            pltpu.VMEM((2 * SWEEPS, SEGS * VECTOR_ROWS, 128), f32),
            pltpu.VMEM((SWEEPS, 2, N, CELLS) + cell, f32),
            pltpu.SemaphoreType.DMA((5,)),
            pltpu.SemaphoreType.DMA((SEGS,)),
            pltpu.SemaphoreType.DMA((SEGS,)),
            pltpu.SemaphoreType.DMA((2 * SWEEPS, SEGS)),
            pltpu.SemaphoreType.DMA((2 * SWEEPS, SEGS)),
            pltpu.SemaphoreType.DMA((SWEEPS, 2)),
            pltpu.SemaphoreType.DMA((SWEEPS, 2)),
        ],
        compiler_params=pltpu.CompilerParams(collective_id=0, has_side_effects=True),
        name="line_relaxation",
    )(state_in, source, face_flux, time_term, inplane_coef)


def solution(mesh):
    return jax.shard_map(
        body,
        mesh=mesh,
        in_specs=(
            P(None, "wall", "band", None),
            P(None, "wall", "band", None),
            P(None, None, "wall", "band", None),
            P(None, "wall", "band", None),
            P(None, "wall", "band", None),
        ),
        out_specs=P(None, "wall", "band", None),
        check_vma=False,
    )
```

time: 330 us -> 45.4 us (0.14)
  the two profiles are of different devices: /device:TPU:25 before, /device:TPU:1 now
where the time goes in v1:
time: 45.4 us; the launch traced here: 45.2 us
  Pallas kernels  43.8 us (96%)
  local copies, waits for them, and re-layouts  1.4 us (3%)
    pallas_call x1, Pallas kernels, body(): pl.pallas_call(kernel, out_shape=jax.ShapeDtypeStruct(state_in.shape, f32...  43.8 us
    unnamed x1, local copies, waits for them, and re-layouts  1.4 us

profile of v1, /device:TPU:1, one launch (start us, length us, event | category | flops | bytes accessed | tf_op | source)
XLA Modules:
  0.0 45.2 jit_solution(17799964506369914813)
XLA Ops:
  0.0 43.8 %line_relaxation.1 = f32[5,8,2,128]{3,2,1,0:T(2,128)} custom-call(f32[5,8,2,128]{3,2,1,0:T(2,128)} %state_in.1, f32[5,8,2,128]{3,2,1,0:T(2,128)} %source_in.1, f32[5,5,8,2,128]{4,3,2,1,0:T(2,128)} %face_in.1, f32[5,8,2,128]{3,2,1,0:T(2,128)} %time_in.1, f32[2,8,2,128]{3,2,1,0:T(2,128)} %coef_in.1), custom_call_target="tpu_custom_call" | custom-call | tf_op jit(solution)/shard_map/line_relaxation/pallas_call | solution.py:430
  43.8 1.4 %copy.7 = f32[5,8,2,128]{3,2,1,0:T(2,128)} copy(f32[5,8,2,128]{3,2,1,0:T(2,128)} %line_relaxation.1) | data formatting | bytes 81920

commit v2 on v1

--- a/solution.py
+++ b/solution.py
@@ -13,7 +13,6 @@
 MATRIX_GROUPS = 13
 VECTOR_GROUPS = 2
 MATRIX_ROWS = 16
-VECTOR_ROWS = 8
 MESH = pl.DeviceIdType.MESH
 
 
@@ -124,17 +123,32 @@
     return tile
 
 
-def pack(fields, messages, groups, rows):
-    for g in range(groups):
+def pack_matrices(fields, messages):
+    for g in range(MATRIX_GROUPS):
         for r in range(2):
             tile = fields[pl.ds(16 * g + r, 8, stride=2), :]
-            messages[pl.ds(8 * r * rows + g, 8, stride=rows), :] = transpose_groups(tile)
-
-
-def unpack(messages, fields, groups, rows):
-    for g in range(groups):
+            rows = pl.ds(8 * r * MATRIX_ROWS + g, 8, stride=MATRIX_ROWS)
+            messages[rows, :] = transpose_groups(tile)
+
+
+def unpack_matrices(messages, fields):
+    for g in range(MATRIX_GROUPS):
         for r in range(2):
-            tile = messages[pl.ds(8 * r * rows + g, 8, stride=rows), :]
+            tile = messages[pl.ds(8 * r * MATRIX_ROWS + g, 8, stride=MATRIX_ROWS), :]
+            fields[pl.ds(16 * g + r, 8, stride=2), :] = transpose_groups(tile)
+
+
+def pack_vectors(fields, messages):
+    for r in range(2):
+        for g in range(VECTOR_GROUPS):
+            tile = fields[pl.ds(16 * g + r, 8, stride=2), :]
+            messages[8 * r : 8 * r + 8, g, :] = transpose_groups(tile)
+
+
+def unpack_vectors(messages, fields):
+    for r in range(2):
+        for g in range(VECTOR_GROUPS):
+            tile = messages[8 * r : 8 * r + 8, g, :]
             fields[pl.ds(16 * g + r, 8, stride=2), :] = transpose_groups(tile)
 
 
@@ -197,12 +211,17 @@
     wall = lax.axis_index("wall")
     band = lax.axis_index("band")
     bands = lax.axis_size("band")
-    band_prev = lax.rem(band + bands - 1, bands)
-    band_next = lax.rem(band + 1, bands)
+    has_prev = band > 0
+    has_next = band < bands - 1
+    neighbours = ((has_next, band + 1), (has_prev, band - 1))
 
     barrier = pltpu.get_barrier_semaphore()
-    for neighbour in (band_prev, band_next):
-        pl.semaphore_signal(barrier, inc=1, device_id={"band": neighbour}, device_id_type=MESH)
+    for present, neighbour in neighbours:
+
+        @pl.when(present)
+        def _():
+            pl.semaphore_signal(barrier, inc=1, device_id={"band": neighbour}, device_id_type=MESH)
+
     for offset in range(1, SEGS):
         pl.semaphore_signal(
             barrier,
@@ -221,13 +240,13 @@
     for load in loads:
         load.start()
 
-    def exchange(send_from, land_in, send_sems, recv_sems, rows):
+    def exchange(send_from, land_in, send_sems, recv_sems, at):
         copies = []
         for offset in range(1, SEGS):
             there = lax.rem(wall + offset, SEGS)
             copy = pltpu.make_async_remote_copy(
-                src_ref=send_from.at[pl.ds(pl.multiple_of(there * rows, rows), rows)],
-                dst_ref=land_in.at[pl.ds(pl.multiple_of(wall * rows, rows), rows)],
+                src_ref=send_from.at[at(there)],
+                dst_ref=land_in.at[at(wall)],
                 send_sem=send_sems.at[offset],
                 recv_sem=recv_sems.at[offset],
                 device_id={"wall": there},
@@ -235,24 +254,39 @@
             )
             copy.start()
             copies.append(copy)
-        own = pl.ds(pl.multiple_of(wall * rows, rows), rows)
-        land_in[own, :] = send_from[own, :]
+        land_in[at(wall)] = send_from[at(wall)]
         return copies
 
-    def exchange_halo(turn):
-        copies = []
-        for side, there in ((0, band_next), (1, band_prev)):
-            copy = pltpu.make_async_remote_copy(
-                src_ref=state,
-                dst_ref=halo_in.at[turn, side],
-                send_sem=halo_send.at[turn, side],
-                recv_sem=halo_recv.at[turn, side],
-                device_id={"band": there},
-                device_id_type=MESH,
-            )
-            copy.start()
-            copies.append(copy)
-        return copies
+    def matrix_at(segment):
+        return pl.ds(pl.multiple_of(segment * MATRIX_ROWS, MATRIX_ROWS), MATRIX_ROWS)
+
+    def vector_at(segment):
+        return segment
+
+    def halo_copy(turn, side):
+        return pltpu.make_async_remote_copy(
+            src_ref=state,
+            dst_ref=halo_in.at[turn, side],
+            send_sem=halo_send.at[turn, side],
+            recv_sem=halo_recv.at[turn, side],
+            device_id={"band": neighbours[side][1]},
+            device_id_type=MESH,
+        )
+
+    def send_halo(turn):
+        for side in range(2):
+
+            @pl.when(neighbours[side][0])
+            def _():
+                halo_copy(turn, side).start()
+
+    def wait_halo(turn):
+        for side in range(2):
+
+            @pl.when(neighbours[side][0])
+            def _():
+                halo_copy(turn, side).wait_send()
+                halo_copy(turn, 1 - side).wait_recv()
 
     for load in loads[:3]:
         load.wait()
@@ -298,20 +332,19 @@
 
     for load in loads[3:]:
         load.wait()
-    pl.semaphore_wait(barrier, SEGS + 1)
-    pending = exchange_halo(0)
-    pack(matrix_fields, matrix_out, MATRIX_GROUPS, MATRIX_ROWS)
-    matrix_copies = exchange(matrix_out, matrix_in, matrix_send, matrix_recv, MATRIX_ROWS)
-
-    has_prev = jnp.where(band > 0, 1.0, 0.0).astype(jnp.float32)
-    has_next = jnp.where(band < bands - 1, 1.0, 0.0).astype(jnp.float32)
+    pl.semaphore_wait(
+        barrier, SEGS - 1 + has_prev.astype(jnp.int32) + has_next.astype(jnp.int32)
+    )
+    send_halo(0)
+    pack_matrices(matrix_fields, matrix_out)
+    matrix_copies = exchange(matrix_out, matrix_in, matrix_send, matrix_recv, matrix_at)
 
     def eliminate(turn):
         value = None
         for m in range(CELLS):
             here = state[:, m]
-            before = halo_in[turn, 0, :, m] * has_prev
-            after = halo_in[turn, 1, :, m] * has_next
+            before = jnp.where(has_prev, halo_in[turn, 0, :, m], 0.0)
+            after = jnp.where(has_next, halo_in[turn, 1, :, m], 0.0)
             top = row_of(here) == 0
             along_i = (1.0 / 12.0) * (before + after) - (4.0 / 3.0) * swap_rows(
                 here + jnp.where(top, after, before)
@@ -377,42 +410,41 @@
         put_vector(vector_fields, N, value)
 
     for turn in range(SWEEPS):
-        for copy in pending:
-            copy.wait()
+        wait_halo(turn)
         eliminate(turn)
         trips = []
         trip = 2 * turn
-        pack(vector_fields, vector_out.at[trip], VECTOR_GROUPS, VECTOR_ROWS)
+        pack_vectors(vector_fields, vector_out.at[trip])
         trips.append(
             exchange(
                 vector_out.at[trip],
                 vector_in.at[trip],
                 vector_send.at[trip],
                 vector_recv.at[trip],
-                VECTOR_ROWS,
+                vector_at,
             )
         )
         if turn == 0:
             for copy in matrix_copies:
                 copy.wait()
-            unpack(matrix_in, matrix_fields, MATRIX_GROUPS, MATRIX_ROWS)
+            unpack_matrices(matrix_in, matrix_fields)
             factor_chain()
         for copy in trips[0]:
             copy.wait()
-        unpack(vector_in.at[trip], vector_fields, VECTOR_GROUPS, VECTOR_ROWS)
+        unpack_vectors(vector_in.at[trip], vector_fields)
         solve_chain()
         trip = trip + 1
-        pack(vector_fields, vector_out.at[trip], VECTOR_GROUPS, VECTOR_ROWS)
+        pack_vectors(vector_fields, vector_out.at[trip])
         answers = exchange(
             vector_out.at[trip],
             vector_in.at[trip],
             vector_send.at[trip],
             vector_recv.at[trip],
-            VECTOR_ROWS,
+            vector_at,
         )
         for copy in answers:
             copy.wait()
-        unpack(vector_in.at[trip], vector_fields, VECTOR_GROUPS, VECTOR_ROWS)
+        unpack_vectors(vector_in.at[trip], vector_fields)
         below = get_vector(vector_fields, 0)
         own = get_vector(vector_fields, N)
         target = out if turn == SWEEPS - 1 else state
@@ -420,7 +452,7 @@
             target[:, m] = partial[m] + matvec(spike_low[m], below) + matvec(spike_high[m], own)
         target[:, INNER] = own
         if turn < SWEEPS - 1:
-            pending = exchange_halo(turn + 1)
+            send_halo(turn + 1)
 
 
 def body(state_in, source, face_flux, time_term, inplane_coef):
@@ -429,7 +461,7 @@
     anywhere = pl.BlockSpec(memory_space=pl.ANY)
     return pl.pallas_call(
         kernel,
-        out_shape=jax.ShapeDtypeStruct(state_in.shape, f32),
+        out_shape=pltpu.VMEM(state_in.shape, f32),
         in_specs=[anywhere] * 5,
         out_specs=pl.BlockSpec(memory_space=pltpu.VMEM),
         scratch_shapes=[
@@ -452,8 +484,8 @@
             pltpu.VMEM((16 * VECTOR_GROUPS, 128), f32),
             pltpu.VMEM((SEGS * MATRIX_ROWS, 128), f32),
             pltpu.VMEM((SEGS * MATRIX_ROWS, 128), f32),
-            pltpu.VMEM((2 * SWEEPS, SEGS * VECTOR_ROWS, 128), f32),
-            pltpu.VMEM((2 * SWEEPS, SEGS * VECTOR_ROWS, 128), f32),
+            pltpu.VMEM((2 * SWEEPS, SEGS, VECTOR_GROUPS, 128), f32),
+            pltpu.VMEM((2 * SWEEPS, SEGS, VECTOR_GROUPS, 128), f32),
             pltpu.VMEM((SWEEPS, 2, N, CELLS) + cell, f32),
             pltpu.SemaphoreType.DMA((5,)),
             pltpu.SemaphoreType.DMA((SEGS,)),

time: 45.4 us -> 40 us (0.88)
  the two profiles are of different devices: /device:TPU:1 before, /device:TPU:25 now
where the time goes in v2:
time: 40 us; the launch traced here: 39.9 us
  Pallas kernels  39.3 us (98%)
  local copies, waits for them, and re-layouts  0.62 us (2%)
    pallas_call x1, Pallas kernels, body(): pl.pallas_call(kernel, out_shape=pltpu.VMEM(state_in.shape, f32), in_spec...  39.3 us

profile of v2, /device:TPU:25, one launch (start us, length us, event | category | flops | bytes accessed | tf_op | source)
XLA Modules:
  0.0 39.9 jit_solution(3990167580789835221)
XLA Ops:
  0.0 39.3 %line_relaxation.1 = f32[5,8,2,128]{3,2,1,0:T(2,128)S(1)} custom-call(f32[5,8,2,128]{3,2,1,0:T(2,128)} %state_in.1, f32[5,8,2,128]{3,2,1,0:T(2,128)} %source_in.1, f32[5,5,8,2,128]{4,3,2,1,0:T(2,128)} %face_in.1, f32[5,8,2,128]{3,2,1,0:T(2,128)} %time_in.1, f32[2,8,2,128]{3,2,1,0:T(2,128)} %coef_in.1), custom_call_target="tpu_custom_call" | custom-call | tf_op jit(solution)/shard_map/line_relaxation/pallas_call | solution.py:462
  39.3 0.6 %copy.7 = f32[5,8,2,128]{3,2,1,0:T(2,128)} copy(f32[5,8,2,128]{3,2,1,0:T(2,128)S(1)} %line_relaxation.1) | data formatting | bytes 81920

commit v3 on v2

--- a/solution.py
+++ b/solution.py
@@ -14,6 +14,7 @@
 VECTOR_GROUPS = 2
 MATRIX_ROWS = 16
 MESH = pl.DeviceIdType.MESH
+FAR_FIRST = sorted(range(1, SEGS), key=lambda offset: -min(offset, SEGS - offset))
 
 
 def matmul(left, right):
@@ -186,8 +187,7 @@
     held_inverse,
     held_lower,
     held_upper,
-    spike_low,
-    spike_high,
+    spikes,
     partial,
     chain_inverse,
     round_inverse,
@@ -200,6 +200,10 @@
     vector_out,
     vector_in,
     halo_in,
+    near_spikes,
+    near_partial,
+    near_answers,
+    near_fields,
     load_sem,
     matrix_send,
     matrix_recv,
@@ -207,7 +211,13 @@
     vector_recv,
     halo_send,
     halo_recv,
+    near_send,
+    near_recv,
+    answer_send,
+    answer_recv,
 ):
+    spike_low = spikes.at[0]
+    spike_high = spikes.at[1]
     wall = lax.axis_index("wall")
     band = lax.axis_index("band")
     bands = lax.axis_size("band")
@@ -242,7 +252,7 @@
 
     def exchange(send_from, land_in, send_sems, recv_sems, at):
         copies = []
-        for offset in range(1, SEGS):
+        for offset in FAR_FIRST:
             there = lax.rem(wall + offset, SEGS)
             copy = pltpu.make_async_remote_copy(
                 src_ref=send_from.at[at(there)],
@@ -255,7 +265,7 @@
             copy.start()
             copies.append(copy)
         land_in[at(wall)] = send_from[at(wall)]
-        return copies
+        return copies[::-1]
 
     def matrix_at(segment):
         return pl.ds(pl.multiple_of(segment * MATRIX_ROWS, MATRIX_ROWS), MATRIX_ROWS)
@@ -287,6 +297,55 @@
             def _():
                 halo_copy(turn, side).wait_send()
                 halo_copy(turn, 1 - side).wait_recv()
+
+    def near_copy(kind, side):
+        source_ref, landing = ((spikes, near_spikes), (partial, near_partial))[kind]
+        return pltpu.make_async_remote_copy(
+            src_ref=source_ref,
+            dst_ref=landing.at[side],
+            send_sem=near_send.at[kind, side],
+            recv_sem=near_recv.at[kind, side],
+            device_id={"band": neighbours[side][1]},
+            device_id_type=MESH,
+        )
+
+    def send_near(kind):
+        for side in range(2):
+
+            @pl.when(neighbours[side][0])
+            def _():
+                near_copy(kind, side).start()
+
+    def answer_copy(answers, side, offset):
+        there = lax.rem(wall + offset, SEGS)
+        return pltpu.make_async_remote_copy(
+            src_ref=answers.at[there],
+            dst_ref=near_answers.at[side, wall],
+            send_sem=answer_send.at[side, offset],
+            recv_sem=answer_recv.at[side, offset],
+            device_id={"band": neighbours[side][1], "wall": there},
+            device_id_type=MESH,
+        )
+
+    def send_answers(answers):
+        for side in range(2):
+
+            @pl.when(neighbours[side][0])
+            def _():
+                for offset in FAR_FIRST + [0]:
+                    answer_copy(answers, side, offset).start()
+
+    def wait_near(answers):
+        for side in range(2):
+
+            @pl.when(neighbours[side][0])
+            def _():
+                for kind in range(2):
+                    near_copy(kind, side).wait_send()
+                    near_copy(kind, 1 - side).wait_recv()
+                for offset in [0] + FAR_FIRST[::-1]:
+                    answer_copy(answers, side, offset).wait_send()
+                    answer_copy(answers, 1 - side, offset).wait_recv()
 
     for load in loads[:3]:
         load.wait()
@@ -338,6 +397,7 @@
     send_halo(0)
     pack_matrices(matrix_fields, matrix_out)
     matrix_copies = exchange(matrix_out, matrix_in, matrix_send, matrix_recv, matrix_at)
+    send_near(0)
 
     def eliminate(turn):
         value = None
@@ -409,32 +469,39 @@
         put_vector(vector_fields, 0, jnp.where(first_segment(before), 0.0, before))
         put_vector(vector_fields, N, value)
 
+    def answer(target, fields, value, low_spike, high_spike):
+        below = get_vector(fields, 0)
+        own = get_vector(fields, N)
+        for m in range(INNER):
+            target[:, m] = value[m] + matvec(low_spike[m], below) + matvec(high_spike[m], own)
+        target[:, INNER] = own
+
+    wait_halo(0)
     for turn in range(SWEEPS):
-        wait_halo(turn)
         eliminate(turn)
-        trips = []
         trip = 2 * turn
         pack_vectors(vector_fields, vector_out.at[trip])
-        trips.append(
-            exchange(
-                vector_out.at[trip],
-                vector_in.at[trip],
-                vector_send.at[trip],
-                vector_recv.at[trip],
-                vector_at,
-            )
+        demands = exchange(
+            vector_out.at[trip],
+            vector_in.at[trip],
+            vector_send.at[trip],
+            vector_recv.at[trip],
+            vector_at,
         )
         if turn == 0:
+            send_near(1)
             for copy in matrix_copies:
                 copy.wait()
             unpack_matrices(matrix_in, matrix_fields)
             factor_chain()
-        for copy in trips[0]:
+        for copy in demands:
             copy.wait()
         unpack_vectors(vector_in.at[trip], vector_fields)
         solve_chain()
         trip = trip + 1
         pack_vectors(vector_fields, vector_out.at[trip])
+        if turn == 0:
+            send_answers(vector_out.at[trip])
         answers = exchange(
             vector_out.at[trip],
             vector_in.at[trip],
@@ -445,14 +512,19 @@
         for copy in answers:
             copy.wait()
         unpack_vectors(vector_in.at[trip], vector_fields)
-        below = get_vector(vector_fields, 0)
-        own = get_vector(vector_fields, N)
-        target = out if turn == SWEEPS - 1 else state
-        for m in range(INNER):
-            target[:, m] = partial[m] + matvec(spike_low[m], below) + matvec(spike_high[m], own)
-        target[:, INNER] = own
-        if turn < SWEEPS - 1:
-            send_halo(turn + 1)
+        answer(out if turn == SWEEPS - 1 else state, vector_fields, partial, spike_low, spike_high)
+        if turn == 0:
+            wait_near(vector_out.at[trip])
+            for side in range(2):
+                fields = near_fields.at[side]
+                unpack_vectors(near_answers.at[side], fields)
+                answer(
+                    halo_in.at[1, side],
+                    fields,
+                    near_partial.at[side],
+                    near_spikes.at[side, 0],
+                    near_spikes.at[side, 1],
+                )
 
 
 def body(state_in, source, face_flux, time_term, inplane_coef):
@@ -473,8 +545,7 @@
             pltpu.VMEM((INNER, N, N) + cell, f32),
             pltpu.VMEM((INNER, N, N) + cell, f32),
             pltpu.VMEM((INNER, N, N) + cell, f32),
-            pltpu.VMEM((INNER, N, N) + cell, f32),
-            pltpu.VMEM((INNER, N, N) + cell, f32),
+            pltpu.VMEM((2, INNER, N, N) + cell, f32),
             pltpu.VMEM((INNER, N) + cell, f32),
             pltpu.VMEM((N, N) + cell, f32),
             pltpu.VMEM((4, N, N) + cell, f32),
@@ -487,6 +558,10 @@
             pltpu.VMEM((2 * SWEEPS, SEGS, VECTOR_GROUPS, 128), f32),
             pltpu.VMEM((2 * SWEEPS, SEGS, VECTOR_GROUPS, 128), f32),
             pltpu.VMEM((SWEEPS, 2, N, CELLS) + cell, f32),
+            pltpu.VMEM((2, 2, INNER, N, N) + cell, f32),
+            pltpu.VMEM((2, INNER, N) + cell, f32),
+            pltpu.VMEM((2, SEGS, VECTOR_GROUPS, 128), f32),
+            pltpu.VMEM((2, 16 * VECTOR_GROUPS, 128), f32),
             pltpu.SemaphoreType.DMA((5,)),
             pltpu.SemaphoreType.DMA((SEGS,)),
             pltpu.SemaphoreType.DMA((SEGS,)),
@@ -494,6 +569,10 @@
             pltpu.SemaphoreType.DMA((2 * SWEEPS, SEGS)),
             pltpu.SemaphoreType.DMA((SWEEPS, 2)),
             pltpu.SemaphoreType.DMA((SWEEPS, 2)),
+            pltpu.SemaphoreType.DMA((2, 2)),
+            pltpu.SemaphoreType.DMA((2, 2)),
+            pltpu.SemaphoreType.DMA((2, SEGS)),
+            pltpu.SemaphoreType.DMA((2, SEGS)),
         ],
         compiler_params=pltpu.CompilerParams(collective_id=0, has_side_effects=True),
         name="line_relaxation",

time: 40 us -> 38.3 us (0.957)
  Pallas kernels: 39.3 us -> 37.4 us
    pallas_call x1, Pallas kernels: 39.3 us -> 37.4 us  [body(): pl.pallas_call(kernel, out_shape=pltpu.VMEM(state_in.shape, f32), in_spec...]
where the time goes in v3:
time: 38.3 us; the launch traced here: 38.1 us
  Pallas kernels  37.4 us (98%)
  local copies, waits for them, and re-layouts  0.62 us (2%)
    pallas_call x1, Pallas kernels, body(): pl.pallas_call(kernel, out_shape=pltpu.VMEM(state_in.shape, f32), in_spec...  37.4 us

profile of v3, /device:TPU:25, one launch (start us, length us, event | category | flops | bytes accessed | tf_op | source)
XLA Modules:
  0.0 38.1 jit_solution(1366720189565165579)
XLA Ops:
  0.0 37.4 %line_relaxation.1 = f32[5,8,2,128]{3,2,1,0:T(2,128)S(1)} custom-call(f32[5,8,2,128]{3,2,1,0:T(2,128)} %state_in.1, f32[5,8,2,128]{3,2,1,0:T(2,128)} %source_in.1, f32[5,5,8,2,128]{4,3,2,1,0:T(2,128)} %face_in.1, f32[5,8,2,128]{3,2,1,0:T(2,128)} %time_in.1, f32[2,8,2,128]{3,2,1,0:T(2,128)} %coef_in.1), custom_call_target="tpu_custom_call" | custom-call | tf_op jit(solution)/shard_map/line_relaxation/pallas_call | solution.py:534
  37.4 0.6 %copy.7 = f32[5,8,2,128]{3,2,1,0:T(2,128)} copy(f32[5,8,2,128]{3,2,1,0:T(2,128)S(1)} %line_relaxation.1) | data formatting | bytes 81920
